TPU v7x, 256 devices: a whole 4x4x8 slice. The times are simulated.
256 devices in a mesh: rows: 64 (over x, z, core), cols: 4 (over y).
Axes of the slice: x: 4, y: 4, z: 8, core: 2. Of those that a mesh axis runs over, the one named last changes fastest.
Arguments:
- slot_tile: int32 [64, 3], replicated, may hold values from 0 to 128, as said below
- slot_ranks: int32 [64, 3, 4], P('rows', None, 'cols'), may hold values from 0 to 256, as said below
- diag_ranks: int32 [4], P('cols'), may hold values from 32 to 256
- panel_left_factors: bfloat16 [4, 192, 1024, 256], P('cols', 'rows'), may hold values from -12 to 12
- panel_v: bfloat16 [4, 192, 1024, 256], P('cols', 'rows'), may hold values from -0.1875 to 0.1875
- diag_u: bfloat16 [4, 1024, 256], P('cols'), may hold values from -0.38 to 0.38, as said below
- diag_v: bfloat16 [4, 1024, 256], P('cols'), may hold values from -1 to 1
- panel_points: int32 [192, 2, 1024], P('rows', None, 'cols'), may hold values from 0 to 1023, as said below
- diag_points: int32 [2, 1024], replicated, may hold values from 0 to 1023, as said below
- rhs_diag: float32 [1024, 512], P(None, 'cols'), may hold values from -0.3 to 0.3
- rhs_rest: float32 [128, 4, 4, 64, 512], P(None, 'cols', None, 'rows'), may hold values from -6 to 6
Outputs:
- panel_factor: bfloat16 [192, 1024, 1024], P('rows', 'cols')
- diag_solution: float32 [1024, 512], P(None, 'cols')
- rhs_out: float32 [128, 4, 4, 64, 512], P(None, 'cols', None, 'rows')
Inputs may be any that keep to these rules, and one draw needn't show every extreme that they name: `slot_tile`: every tile 0 to 127 stands in exactly one slot; 128 marks an empty slot; the live slots of an owner come first; every owner has 1 to 3 live slots and some owner has 3. Owners are chosen by the tiles' summed ranks. `slot_ranks`: live slots have ranks 32 to 256, empty slots 0; both 32 and 256 occur. The columns of each diag_u[j] are orthogonal, with lengths 0.1 to 0.38. `panel_points`: row 0 holds x, row 1 holds y. A live slot holds the cells of a block of 32 x (32) grid cells in some order; blocks of different tiles and of the diagonal tile are distinct; an empty slot holds the points of some tile. `diag_points`: row 0 holds x, row 1 holds y: the cells of one block of 32 x (32) grid cells in some order.
All inputs are finite; a program needn't handle non-finite values.
Results may differ from a plain program's by a relative error of at most 0.0057.
Values may be sent and summed in bfloat16 or wider, within the bound.
A program may use at most 128 MiB of HBM per device.

v0:
```python
import jax
import jax.numpy as jnp
from jax import lax
from jax.sharding import PartitionSpec as P

GX = 1024
length_scale = 0.3
nugget = 1.0


def matern(first_x, first_y, second_x, second_y):
    spacing = 1.0 / GX
    delta_x = (first_x - second_x) * spacing
    delta_y = (first_y - second_y) * spacing
    scaled = jnp.sqrt(3.0) * jnp.sqrt(delta_x * delta_x + delta_y * delta_y) / length_scale
    return (1.0 + scaled) * jnp.exp(-scaled)


def owner_rows(slot_tile, tile_count, per_peer, row_devices):
    flat_tiles = slot_tile.reshape(-1)
    slot_count = flat_tiles.shape[0]
    tmax_local = slot_tile.shape[1]
    owner_slot = (
        jnp.zeros((tile_count + 1,), jnp.int32)
        .at[flat_tiles]
        .set(jnp.arange(slot_count, dtype=jnp.int32))[:tile_count]
    )
    source_row = owner_slot // tmax_local
    source_place = owner_slot % tmax_local
    step_index = jnp.arange(per_peer, dtype=jnp.int32)
    return (
        (source_place[:, None] * per_peer + step_index[None, :]) * row_devices + source_row[:, None]
    ).reshape(-1)


def times_block(owned_rows, forward):
    return jnp.dot(
        owned_rows,
        lax.all_gather(forward, "cols", axis=1, tiled=True),
        preferred_element_type=jnp.float32,
    )


def per_device(
    slot_tile,
    slot_ranks,
    diag_ranks,
    panel_left_factors,
    panel_v,
    diag_u,
    diag_v,
    panel_points,
    diag_points,
    rhs_diag,
    rhs_rest,
):
    row_devices = lax.axis_size("rows")
    col_devices = lax.axis_size("cols")
    slot_count = panel_left_factors.shape[1]
    tile_order = diag_u.shape[1]
    rank_max = diag_u.shape[2]
    quarter = tile_order // col_devices
    per_peer = quarter // row_devices
    tile_count = rhs_rest.shape[0]
    row_index = lax.axis_index("rows")
    rank_index = jnp.arange(rank_max, dtype=jnp.int32)
    diag_mask = (rank_index < diag_ranks[0]).astype(jnp.bfloat16)
    diagonal_left_factor = diag_u[0] * diag_mask[None, :]
    diagonal_right_factor = diag_v[0] * diag_mask[None, :]
    slot_mask = (rank_index[None, :] < slot_ranks[0, :, 0][:, None]).astype(jnp.bfloat16)
    slot_left_factor = panel_left_factors[0] * slot_mask[:, None, :]
    slot_right_factor = panel_v[0] * slot_mask[:, None, :]
    inner_product_core = jnp.einsum(
        "gok,oe->gke", slot_right_factor, diagonal_right_factor, preferred_element_type=jnp.float32
    ).astype(jnp.bfloat16)
    low_rows = jnp.einsum(
        "lgc,lcz->lgz", slot_left_factor, inner_product_core, preferred_element_type=jnp.float32
    ).astype(jnp.bfloat16)
    diag_core = jnp.einsum(
        "br,bq->rq",
        diagonal_right_factor,
        diagonal_right_factor,
        preferred_element_type=jnp.float32,
    ).astype(jnp.bfloat16)
    diag_low = jnp.dot(diagonal_left_factor, diag_core, preferred_element_type=jnp.float32).astype(
        jnp.bfloat16
    )
    gathered_low, gathered_left = (
        lax.all_gather(diag_low[None], "cols", axis=0, tiled=True),
        lax.all_gather(diagonal_left_factor[None], "cols", axis=0, tiled=True),
    )
    outgoing_low = low_rows.reshape(slot_count, col_devices, quarter, rank_max)
    update_term = jnp.einsum(
        "sjnr,jbr->snb",
        lax.all_to_all(outgoing_low, "cols", split_axis=1, concat_axis=1, tiled=True),
        gathered_left,
        preferred_element_type=jnp.float32,
    )
    centre = diag_points.astype(jnp.float32)
    identity = jnp.eye(tile_order, dtype=jnp.float32)
    diag_term = jnp.einsum(
        "jbr,jcr->bc", gathered_low, gathered_left, preferred_element_type=jnp.float32
    )
    own_block = matern(centre[0][:, None], centre[1][:, None], centre[0], centre[1])
    diag_system = own_block + nugget * identity - diag_term
    factor = jnp.linalg.cholesky(diag_system)
    inverse = jax.scipy.linalg.solve_triangular(factor, identity, lower=True)
    my_tiles = lax.dynamic_slice_in_dim(slot_tile, row_index, 1, 0)[0]
    live_mask = (my_tiles < tile_count).astype(jnp.float32)
    coords = panel_points.astype(jnp.float32)
    generated = matern(coords[:, 0, :, None], coords[:, 1, :, None], centre[0], centre[1])
    system_rows = live_mask[:, None, None] * (generated - update_term)
    panel_factor = jnp.einsum(
        "snb,cb->snc", system_rows, inverse, precision=lax.Precision.HIGHEST
    ).astype(jnp.bfloat16)
    diag_solution = jnp.dot(inverse, rhs_diag, precision=lax.Precision.HIGHEST)
    forward = diag_solution.astype(jnp.bfloat16)
    pick_rows = owner_rows(slot_tile, tile_count, per_peer, row_devices)
    outgoing_rows = panel_factor.reshape(slot_count, per_peer, row_devices, tile_order)
    incoming = lax.all_to_all(outgoing_rows, "rows", split_axis=2, concat_axis=2, tiled=True)
    owned_rows = jnp.take(incoming.reshape(-1, tile_order), pick_rows, axis=0)
    product = times_block(owned_rows, forward).astype(jnp.bfloat16)
    rhs_out = rhs_rest - product.reshape(rhs_rest.shape).astype(jnp.float32)
    return (panel_factor, diag_solution, rhs_out)


def solution(mesh):
    return jax.shard_map(
        per_device,
        mesh=mesh,
        in_specs=(
            P(),
            P("rows", None, "cols"),
            P("cols"),
            P("cols", "rows", None, None),
            P("cols", "rows", None, None),
            P("cols", None, None),
            P("cols", None, None),
            P("rows", None, "cols"),
            P(),
            P(None, "cols"),
            P(None, "cols", None, "rows", None),
        ),
        out_specs=(P("rows", "cols", None), P(None, "cols"), P(None, "cols", None, "rows", None)),
        check_vma=False,
    )
```

profile of v0, /device:TPU:1, one launch (start us, length us, event | category | flops | bytes accessed | tf_op | source)
XLA Modules:
  0.0 559.6 jit_solution(14840995524542032224)
XLA Ops:
  27.1 34.0 %all-gather.5.cloned.1.call-done = bf16[4,1024,256]{2,1,0:T(8,128)(2,1)} async-done(((bf16[1,1024,256]{2,1,0:T(8,128)(2,1)}), bf16[4,1024,256]{2,1,0:T(8,128)(2,1)}) %all-gather.5.cloned.1.call-update) | async-done | bytes 2097168 | tf_op jit(solution)/shard_map/all_gather | solution.py:90
  61.1 36.7 %all-gather.9.cloned.1.call-done = bf16[4096,256]{1,0:T(8,128)(2,1)} async-done(((bf16[1024,256]{1,0:T(8,128)(2,1)}), bf16[4096,256]{1,0:T(8,128)(2,1)}) %all-gather.9.cloned.1.call-update) | async-done | bytes 2097168 | tf_op jit(solution)/shard_map/all_gather | solution.py:89
  97.8 6.6 %convolution_bitcast_fusion = f32[1024,1024]{1,0:T(8,128)} fusion(bf16[4,1024,256]{2,1,0:T(8,128)(2,1)} %bitcast.174, bf16[4,1024,256]{2,1,0:T(8,128)(2,1)} %all-gather.5.cloned.1.call-done), kind=kOutput, calls=%fused_computation.28 | convolution fusion | flops 2147483648 | bytes 8388608 | tf_op jit(solution)/shard_map/jbr,jcr->bc/dot_general | solution.py:101
  109.7 9.6 %fusion.3 = f32[1024,1024]{1,0:T(8,128)S(1)} fusion(f32[1024,1024]{0,1:T(8,128)} %copy.22, f32[1024,1024]{1,0:T(8,128)} %convolution_bitcast_fusion, f32[1024]{0:T(1024)S(1)} %bitcast.169, f32[1024]{0:T(1024)S(1)} %bitcast.167), kind=kLoop, calls=%fused_computation.9 | loop fusion | flops 33554432 | bytes 12591104 | tf_op jit(solution)/shard_map/jit(cholesky)/div | solution.py:106
  121.3 11.7 %cholesky.224 = f32[128,128]{1,0:T(8,128)S(1)} custom-call(f32[128,128]{1,0:T(8,128)S(1)} %cholesky.583), custom_call_target="Cholesky" | custom-call | tf_op jit(solution)/shard_map/jit(cholesky)/cholesky | solution.py:106
  133.0 9.8 %custom-call.63 = f32[1,128,128]{1,2,0:T(8,128)S(1)} custom-call(f32[1,128,128]{2,1,0:T(8,128)S(1)} %get-tuple-element.67), custom_call_target="InvertDiagBlocksLowerTriangular" | custom-call | tf_op jit(solution)/shard_map/jit(cholesky)/cholesky | solution.py:106
  149.3 11.7 %cholesky.245 = f32[128,128]{1,0:T(8,128)S(1)} custom-call(f32[128,128]{1,0:T(8,128)S(1)} %cholesky.587), custom_call_target="Cholesky" | custom-call | tf_op jit(solution)/shard_map/jit(cholesky)/cholesky | solution.py:106
  161.6 10.2 %custom-call.64 = f32[1,128,128]{1,2,0:T(8,128)S(1)} custom-call(f32[1,128,128]{2,1,0:T(8,128)S(1)} %get-tuple-element.64), custom_call_target="InvertDiagBlocksLowerTriangular" | custom-call | tf_op jit(solution)/shard_map/jit(cholesky)/cholesky | solution.py:106
  175.2 11.7 %cholesky.470 = f32[128,128]{1,0:T(8,128)S(1)} custom-call(f32[128,128]{1,0:T(8,128)S(1)} %cholesky.592), custom_call_target="Cholesky" | custom-call | tf_op jit(solution)/shard_map/jit(cholesky)/cholesky | solution.py:106
  188.3 9.8 %custom-call.65 = f32[1,128,128]{1,2,0:T(8,128)S(1)} custom-call(f32[1,128,128]{2,1,0:T(8,128)S(1)} %get-tuple-element.61), custom_call_target="InvertDiagBlocksLowerTriangular" | custom-call | tf_op jit(solution)/shard_map/jit(cholesky)/cholesky | solution.py:106
  201.6 11.9 %cholesky.489 = f32[128,128]{1,0:T(8,128)S(1)} custom-call(f32[128,128]{1,0:T(8,128)S(1)} %cholesky.597), custom_call_target="Cholesky" | custom-call | tf_op jit(solution)/shard_map/jit(cholesky)/cholesky | solution.py:106
  214.8 9.8 %custom-call.66 = f32[1,128,128]{1,2,0:T(8,128)S(1)} custom-call(f32[1,128,128]{2,1,0:T(8,128)S(1)} %get-tuple-element.58), custom_call_target="InvertDiagBlocksLowerTriangular" | custom-call | tf_op jit(solution)/shard_map/jit(cholesky)/cholesky | solution.py:106
  228.1 11.7 %cholesky.508 = f32[128,128]{1,0:T(8,128)S(1)} custom-call(f32[128,128]{1,0:T(8,128)S(1)} %cholesky.602), custom_call_target="Cholesky" | custom-call | tf_op jit(solution)/shard_map/jit(cholesky)/cholesky | solution.py:106
  241.1 9.8 %custom-call.67 = f32[1,128,128]{1,2,0:T(8,128)S(1)} custom-call(f32[1,128,128]{2,1,0:T(8,128)S(1)} %get-tuple-element.55), custom_call_target="InvertDiagBlocksLowerTriangular" | custom-call | tf_op jit(solution)/shard_map/jit(cholesky)/cholesky | solution.py:106
  254.4 11.7 %cholesky.528 = f32[128,128]{1,0:T(8,128)S(1)} custom-call(f32[128,128]{1,0:T(8,128)S(1)} %cholesky.607), custom_call_target="Cholesky" | custom-call | tf_op jit(solution)/shard_map/jit(cholesky)/cholesky | solution.py:106
  267.5 9.8 %custom-call.68 = f32[1,128,128]{1,2,0:T(8,128)S(1)} custom-call(f32[1,128,128]{2,1,0:T(8,128)S(1)} %get-tuple-element.52), custom_call_target="InvertDiagBlocksLowerTriangular" | custom-call | tf_op jit(solution)/shard_map/jit(cholesky)/cholesky | solution.py:106
  280.3 11.7 %cholesky.548 = f32[128,128]{1,0:T(8,128)S(1)} custom-call(f32[128,128]{1,0:T(8,128)S(1)} %cholesky.612), custom_call_target="Cholesky" | custom-call | tf_op jit(solution)/shard_map/jit(cholesky)/cholesky | solution.py:106
  293.3 10.2 %custom-call.69 = f32[1,128,128]{1,2,0:T(8,128)S(1)} custom-call(f32[1,128,128]{2,1,0:T(8,128)S(1)} %get-tuple-element.49), custom_call_target="InvertDiagBlocksLowerTriangular" | custom-call | tf_op jit(solution)/shard_map/jit(cholesky)/cholesky | solution.py:106
  306.2 11.7 %cholesky.566 = f32[128,128]{1,0:T(8,128)S(1)} custom-call(f32[128,128]{1,0:T(8,128)S(1)} %convolution_subtract_fusion.11), custom_call_target="Cholesky" | custom-call | tf_op jit(solution)/shard_map/jit(cholesky)/cholesky | solution.py:106
  329.7 27.4 %while.1 = (s32[]{:T(128)}, f32[1024,1024]{1,0:T(8,128)}, s32[8,2]{0,1:T(2,128)S(1)}, f32[8,128,128]{2,1,0:T(8,128)}, s32[]{:T(128)}) while((s32[]{:T(128)}, f32[1024,1024]{1,0:T(8,128)}, s32[8,2]{0,1:T(2,128)S(1)}, f32[8,128,128]{2,1,0:T(8,128)}, s32[]{:T(128)}) %tuple.66), condition=%wide.while_cond, body=%wide.while_body.sunk | while | flops 2 | bytes 132705 | solution.py:107
  357.1 79.6 %custom-call.70 = f32[8,128,128]{1,2,0:T(8,128)S(1)} custom-call(f32[8,128,128]{2,1,0:T(8,128)} %get-tuple-element.10), custom_call_target="InvertDiagBlocksLowerTriangular" | custom-call | tf_op jit(solution)/shard_map/jit(_solve_triangular)/triangular_solve | solution.py:107
  469.6 16.3 %fusion.29 = bf16[3,256,1024]{2,1,0:T(8,128)(2,1)S(1)} fusion(f32[1024,1024]{1,0:T(8,128)} %convolution_dynamic-update-slice_fusion, f32[3,256,1024,1]{2,1,0,3:T(8,128)S(1)} %fusion.27, f32[1024]{0:T(1024)S(1)} %bitcast.170, f32[3,256]{1,0:T(4,128)S(1)} %get-tuple-element.84, f32[1024]{0:T(1024)S(1)} %bitcast.168, f32[3,256]{1,0:T(4,128)S(1)} %get-tuple-element.85, ...), kind=kOutput, calls=%fused_computation.40 | convolution fusion | flops 9674686464 | bytes 8927244 | tf_op jit(solution)/shard_map/snb,cb->snc/dot_general | solution.py:113
  489.4 11.0 %all-to-all-start.1 = ((bf16[3,4,64,1024]{3,1,0,2:T(4,128)(2,1)}), bf16[3,4,64,1024]{3,1,0,2:T(4,128)(2,1)}, u32[]{:S(2)}, u32[]{:S(2)}) async-start(bf16[3,4,64,1024]{3,1,0,2:T(4,128)(2,1)} %copy.24), calls=%async_computation.1 | async-start | bytes 3145728 | tf_op jit(solution)/shard_map/all_to_all | solution.py:120
  509.0 31.1 %all-to-all-done.1 = bf16[3,4,64,1024]{3,1,0,2:T(4,128)(2,1)} async-done(((bf16[3,4,64,1024]{3,1,0,2:T(4,128)(2,1)}), bf16[3,4,64,1024]{3,1,0,2:T(4,128)(2,1)}, u32[]{:S(2)}, u32[]{:S(2)}) %all-to-all-start.1) | async-done | bytes 1572896 | tf_op jit(solution)/shard_map/all_to_all | solution.py:120
  (144 shorter events, 151.1 us)
Async XLA Ops:
  7.2 493.5 %copy-start = (f32[1024,128]{1,0:T(8,128)S(1)}, f32[1024,128]{1,0:T(8,128)}, u32[]{:S(2)}) copy-start(f32[1024,128]{1,0:T(8,128)} %param.20) | copy-start | bytes 1572868
  7.2 5.9 %copy-start.9 = (bf16[1,1024,256]{2,1,0:T(8,128)(2,1)S(1)}, bf16[1,1024,256]{2,1,0:T(8,128)(2,1)}, u32[]{:S(2)}) copy-start(bf16[1,1024,256]{2,1,0:T(8,128)(2,1)} %param.17) | copy-start | bytes 1572868
  7.2 5.8 %copy-start.8 = (s32[1,3,1]{1,2,0:T(1,128)S(1)}, s32[1,3,1]{1,2,0:T(1,128)}, u32[]{:S(2)}) copy-start(s32[1,3,1]{1,2,0:T(1,128)} %param.12) | copy-start | bytes 40
  7.2 53.9 %all-gather.5.cloned.1.call-start = ((), (), s32[]{:S(2)}) async-start(), calls=%async_computation.2 | async-start | bytes 2621440 | tf_op jit(solution)/shard_map/all_gather | solution.py:90
  9.9 87.9 %all-gather.9.cloned.1.call-start = ((), (), s32[]{:S(2)}) async-start(), calls=%async_computation.4 | async-start | bytes 2621440 | tf_op jit(solution)/shard_map/all_gather | solution.py:89
  16.8 6.3 %copy-start.6 = (s32[2,1024]{1,0:T(2,128)S(1)}, s32[2,1024]{1,0:T(2,128)}, u32[]{:S(2)}) copy-start(s32[2,1024]{1,0:T(2,128)} %param.19) | copy-start | bytes 24580
  16.8 6.3 %copy-start.7 = (s32[3,2,256]{2,1,0:T(2,128)S(1)}, s32[3,2,256]{2,1,0:T(2,128)}, u32[]{:S(2)}) copy-start(s32[3,2,256]{2,1,0:T(2,128)} %param.18) | copy-start | bytes 18436
  16.8 6.3 %copy-start.5 = (s32[64,3]{0,1:T(4,128)S(1)}, s32[64,3]{0,1:T(4,128)}, u32[]{:S(2)}) copy-start(s32[64,3]{0,1:T(4,128)} %param.11) | copy-start | bytes 2308
  18.1 448.1 %all-to-all-start = ((bf16[3,4,256,256]{3,2,0,1:T(8,128)(2,1)}), bf16[3,4,256,256]{3,2,0,1:T(8,128)(2,1)S(1)}, u32[]{:S(2)}, u32[]{:S(2)}) async-start(bf16[3,4,256,256]{3,2,0,1:T(8,128)(2,1)} %copy.20), calls=%async_computation | async-start | bytes 3145728 | tf_op jit(solution)/shard_map/all_to_all | solution.py:95
  119.3 2.0 copy-start.2
  436.7 5.6 %copy-start.1 = (f32[1024,1024]{1,0:T(8,128)S(1)}, f32[1024,1024]{1,0:T(8,128)}, u32[]{:S(2)}) copy-start(f32[1024,1024]{1,0:T(8,128)} %fusion.42) | copy-start | bytes 12582916
  485.9 1.1 copy-start.3
  489.4 50.7 %all-to-all-start.1 = ((bf16[3,4,64,1024]{3,1,0,2:T(4,128)(2,1)}), bf16[3,4,64,1024]{3,1,0,2:T(4,128)(2,1)}, u32[]{:S(2)}, u32[]{:S(2)}) async-start(bf16[3,4,64,1024]{3,1,0,2:T(4,128)(2,1)} %copy.24), calls=%async_computation.1 | async-start | bytes 3145728 | tf_op jit(solution)/shard_map/all_to_all | solution.py:120
  500.4 44.4 %all-gather.7.cloned.1.call-start = ((), (), s32[]{:S(2)}) async-start(), calls=%async_computation.3 | async-start | bytes 1310720 | tf_op jit(solution)/shard_map/all_gather | solution.py:39
  544.7 5.9 %copy-start.4 = (f32[128,1,4,1,512]{4,3,2,1,0:T(1,128)S(1)}, f32[128,1,4,1,512]{4,3,2,1,0:T(1,128)}, u32[]{:S(2)}) copy-start(f32[128,1,4,1,512]{4,3,2,1,0:T(1,128)} %param.21) | copy-start | bytes 3145732
Sparse Core Ops, SparseCore 0:
  10.0 51.0 all-gather.4
  63.5 34.2 all-gather.8
  507.3 26.3 all-gather.6
where the time goes:
time: 567 us; the launch traced here: 560 us
  other arithmetic  275 us (49%)
  waiting for transfers between devices  102 us (18%)
  matrix products  95.5 us (17%)
  local copies, waits for them, and re-layouts  50.8 us (9%)
  between operations  20.4 us (4%)
  starting transfers between devices  16.4 us (3%)
    another operation x30, other arithmetic, per_device(): factor = jnp.linalg.cholesky(diag_system)  172 us
    another operation x3, other arithmetic, per_device(): inverse = jax.scipy.linalg.solve_triangular(factor, identity, lower=True)  84.4 us
    all_gather x1, waiting for transfers between devices, per_device(): lax.all_gather(diag_low[None], 'cols', axis=0, tiled=True)  36.7 us
    all_gather x1, waiting for transfers between devices, per_device(): lax.all_gather(diagonal_left_factor[None], 'cols', axis=0, tiled=True)  34 us
    all_to_all x1, waiting for transfers between devices, per_device(): lax.all_to_all(outgoing_rows, 'rows', split_axis=2, concat_axis=2, tiled=...  31.1 us
    another operation x15, matrix products, per_device(): inverse = jax.scipy.linalg.solve_triangular(factor, identity, lower=True)  29.4 us
    another operation x24, local copies, waits for them, and re-layouts  27.4 us
    another operation x14, matrix products, per_device(): factor = jnp.linalg.cholesky(diag_system)  23.3 us
  transfers between devices with their start and end apart: 5, of which 3 were waited for; matrix products, arithmetic and copies ran while one was open for 69% of the time, Pallas kernels for 0%

commit v1 on v0

--- a/solution.py
+++ b/solution.py
@@ -117,7 +117,11 @@
     forward = diag_solution.astype(jnp.bfloat16)
     pick_rows = owner_rows(slot_tile, tile_count, per_peer, row_devices)
     outgoing_rows = panel_factor.reshape(slot_count, per_peer, row_devices, tile_order)
-    incoming = lax.all_to_all(outgoing_rows, "rows", split_axis=2, concat_axis=2, tiled=True)
+    vec_out = lax.axis_size("rows")
+    state_now = jnp.split(outgoing_rows, vec_out, 2)
+    small = jnp.stack(state_now)
+    near = lax.all_to_all(small, "rows", 0, 0)
+    incoming = jnp.concatenate(near, 2)
     owned_rows = jnp.take(incoming.reshape(-1, tile_order), pick_rows, axis=0)
     product = times_block(owned_rows, forward).astype(jnp.bfloat16)
     rhs_out = rhs_rest - product.reshape(rhs_rest.shape).astype(jnp.float32)

time: 567 us -> 608 us (1.072)
  local copies, waits for them, and re-layouts: 50.8 us -> 91.7 us
    unnamed x22 -> x87, local copies, waits for them, and re-layouts: 3.25 us -> 42.1 us
    another operation x24 -> x25, local copies, waits for them, and re-layouts: 27.4 us -> 28 us
  transfers between devices with their start and end apart: 5 -> 5, of which waited for: 3 -> 3; matrix products, arithmetic and copies ran while one was open for 69% -> 64% of each run, Pallas kernels for 0% -> 0%
where the time goes in v1:
time: 608 us; the launch traced here: 601 us
  other arithmetic  275 us (45%)
  waiting for transfers between devices  102 us (17%)
  matrix products  95.8 us (16%)
  local copies, waits for them, and re-layouts  91.7 us (15%)
  between operations  20.6 us (3%)
  starting transfers between devices  15.9 us (3%)
    another operation x30, other arithmetic, per_device(): factor = jnp.linalg.cholesky(diag_system)  172 us
    another operation x3, other arithmetic, per_device(): inverse = jax.scipy.linalg.solve_triangular(factor, identity, lower=True)  84.4 us
    unnamed x87, local copies, waits for them, and re-layouts  42.1 us
    all_gather x1, waiting for transfers between devices, per_device(): lax.all_gather(diag_low[None], 'cols', axis=0, tiled=True)  36.7 us
    all_gather x1, waiting for transfers between devices, per_device(): lax.all_gather(diagonal_left_factor[None], 'cols', axis=0, tiled=True)  34 us
    all_to_all x1, waiting for transfers between devices, per_device(): near = lax.all_to_all(small, 'rows', 0, 0)  31.4 us
    another operation x15, matrix products, per_device(): inverse = jax.scipy.linalg.solve_triangular(factor, identity, lower=True)  29.4 us
    another operation x24, local copies, waits for them, and re-layouts  27.4 us
  transfers between devices with their start and end apart: 5, of which 3 were waited for; matrix products, arithmetic and copies ran while one was open for 64% of the time, Pallas kernels for 0%

profile of v1, /device:TPU:1, one launch (start us, length us, event | category | flops | bytes accessed | tf_op | source)
XLA Modules:
  0.0 600.7 jit_solution(14431370827330873191)
XLA Ops:
  27.1 34.0 %all-gather.5.cloned.1.call-done = bf16[4,1024,256]{2,1,0:T(8,128)(2,1)} async-done(((bf16[1,1024,256]{2,1,0:T(8,128)(2,1)}), bf16[4,1024,256]{2,1,0:T(8,128)(2,1)}) %all-gather.5.cloned.1.call-update) | async-done | bytes 2097168 | tf_op jit(solution)/shard_map/all_gather | solution.py:90
  61.1 36.7 %all-gather.9.cloned.1.call-done = bf16[4096,256]{1,0:T(8,128)(2,1)} async-done(((bf16[1024,256]{1,0:T(8,128)(2,1)}), bf16[4096,256]{1,0:T(8,128)(2,1)}) %all-gather.9.cloned.1.call-update) | async-done | bytes 2097168 | tf_op jit(solution)/shard_map/all_gather | solution.py:89
  97.8 6.6 %convolution_bitcast_fusion = f32[1024,1024]{1,0:T(8,128)} fusion(bf16[4,1024,256]{2,1,0:T(8,128)(2,1)} %bitcast.435, bf16[4,1024,256]{2,1,0:T(8,128)(2,1)} %all-gather.5.cloned.1.call-done), kind=kOutput, calls=%fused_computation.28 | convolution fusion | flops 2147483648 | bytes 8388608 | tf_op jit(solution)/shard_map/jbr,jcr->bc/dot_general | solution.py:101
  109.7 9.6 %fusion.3 = f32[1024,1024]{1,0:T(8,128)S(1)} fusion(f32[1024,1024]{0,1:T(8,128)} %copy.151, f32[1024,1024]{1,0:T(8,128)} %convolution_bitcast_fusion, f32[1024]{0:T(1024)S(1)} %bitcast.430, f32[1024]{0:T(1024)S(1)} %bitcast.428), kind=kLoop, calls=%fused_computation.9 | loop fusion | flops 33554432 | bytes 12591104 | tf_op jit(solution)/shard_map/jit(cholesky)/div | solution.py:106
  121.3 11.7 %cholesky.224 = f32[128,128]{1,0:T(8,128)S(1)} custom-call(f32[128,128]{1,0:T(8,128)S(1)} %cholesky.583), custom_call_target="Cholesky" | custom-call | tf_op jit(solution)/shard_map/jit(cholesky)/cholesky | solution.py:106
  133.0 9.8 %custom-call.63 = f32[1,128,128]{1,2,0:T(8,128)S(1)} custom-call(f32[1,128,128]{2,1,0:T(8,128)S(1)} %get-tuple-element.131), custom_call_target="InvertDiagBlocksLowerTriangular" | custom-call | tf_op jit(solution)/shard_map/jit(cholesky)/cholesky | solution.py:106
  149.3 11.7 %cholesky.245 = f32[128,128]{1,0:T(8,128)S(1)} custom-call(f32[128,128]{1,0:T(8,128)S(1)} %cholesky.587), custom_call_target="Cholesky" | custom-call | tf_op jit(solution)/shard_map/jit(cholesky)/cholesky | solution.py:106
  161.6 10.2 %custom-call.64 = f32[1,128,128]{1,2,0:T(8,128)S(1)} custom-call(f32[1,128,128]{2,1,0:T(8,128)S(1)} %get-tuple-element.128), custom_call_target="InvertDiagBlocksLowerTriangular" | custom-call | tf_op jit(solution)/shard_map/jit(cholesky)/cholesky | solution.py:106
  175.2 11.7 %cholesky.470 = f32[128,128]{1,0:T(8,128)S(1)} custom-call(f32[128,128]{1,0:T(8,128)S(1)} %cholesky.592), custom_call_target="Cholesky" | custom-call | tf_op jit(solution)/shard_map/jit(cholesky)/cholesky | solution.py:106
  188.3 9.8 %custom-call.65 = f32[1,128,128]{1,2,0:T(8,128)S(1)} custom-call(f32[1,128,128]{2,1,0:T(8,128)S(1)} %get-tuple-element.125), custom_call_target="InvertDiagBlocksLowerTriangular" | custom-call | tf_op jit(solution)/shard_map/jit(cholesky)/cholesky | solution.py:106
  201.6 11.9 %cholesky.489 = f32[128,128]{1,0:T(8,128)S(1)} custom-call(f32[128,128]{1,0:T(8,128)S(1)} %cholesky.597), custom_call_target="Cholesky" | custom-call | tf_op jit(solution)/shard_map/jit(cholesky)/cholesky | solution.py:106
  214.8 9.8 %custom-call.66 = f32[1,128,128]{1,2,0:T(8,128)S(1)} custom-call(f32[1,128,128]{2,1,0:T(8,128)S(1)} %get-tuple-element.122), custom_call_target="InvertDiagBlocksLowerTriangular" | custom-call | tf_op jit(solution)/shard_map/jit(cholesky)/cholesky | solution.py:106
  228.1 11.7 %cholesky.508 = f32[128,128]{1,0:T(8,128)S(1)} custom-call(f32[128,128]{1,0:T(8,128)S(1)} %cholesky.602), custom_call_target="Cholesky" | custom-call | tf_op jit(solution)/shard_map/jit(cholesky)/cholesky | solution.py:106
  241.1 9.8 %custom-call.67 = f32[1,128,128]{1,2,0:T(8,128)S(1)} custom-call(f32[1,128,128]{2,1,0:T(8,128)S(1)} %get-tuple-element.119), custom_call_target="InvertDiagBlocksLowerTriangular" | custom-call | tf_op jit(solution)/shard_map/jit(cholesky)/cholesky | solution.py:106
  254.4 11.7 %cholesky.528 = f32[128,128]{1,0:T(8,128)S(1)} custom-call(f32[128,128]{1,0:T(8,128)S(1)} %cholesky.607), custom_call_target="Cholesky" | custom-call | tf_op jit(solution)/shard_map/jit(cholesky)/cholesky | solution.py:106
  267.5 9.8 %custom-call.68 = f32[1,128,128]{1,2,0:T(8,128)S(1)} custom-call(f32[1,128,128]{2,1,0:T(8,128)S(1)} %get-tuple-element.116), custom_call_target="InvertDiagBlocksLowerTriangular" | custom-call | tf_op jit(solution)/shard_map/jit(cholesky)/cholesky | solution.py:106
  280.3 11.7 %cholesky.548 = f32[128,128]{1,0:T(8,128)S(1)} custom-call(f32[128,128]{1,0:T(8,128)S(1)} %cholesky.612), custom_call_target="Cholesky" | custom-call | tf_op jit(solution)/shard_map/jit(cholesky)/cholesky | solution.py:106
  293.3 10.2 %custom-call.69 = f32[1,128,128]{1,2,0:T(8,128)S(1)} custom-call(f32[1,128,128]{2,1,0:T(8,128)S(1)} %get-tuple-element.113), custom_call_target="InvertDiagBlocksLowerTriangular" | custom-call | tf_op jit(solution)/shard_map/jit(cholesky)/cholesky | solution.py:106
  306.2 11.7 %cholesky.566 = f32[128,128]{1,0:T(8,128)S(1)} custom-call(f32[128,128]{1,0:T(8,128)S(1)} %convolution_subtract_fusion.11), custom_call_target="Cholesky" | custom-call | tf_op jit(solution)/shard_map/jit(cholesky)/cholesky | solution.py:106
  329.7 27.4 %while.1 = (s32[]{:T(128)}, f32[1024,1024]{1,0:T(8,128)}, s32[8,2]{0,1:T(2,128)S(1)}, f32[8,128,128]{2,1,0:T(8,128)}, s32[]{:T(128)}) while((s32[]{:T(128)}, f32[1024,1024]{1,0:T(8,128)}, s32[8,2]{0,1:T(2,128)S(1)}, f32[8,128,128]{2,1,0:T(8,128)}, s32[]{:T(128)}) %tuple.126), condition=%wide.while_cond, body=%wide.while_body.sunk | while | flops 2 | bytes 132705 | solution.py:107
  357.1 79.6 %custom-call.70 = f32[8,128,128]{1,2,0:T(8,128)S(1)} custom-call(f32[8,128,128]{2,1,0:T(8,128)} %get-tuple-element.10), custom_call_target="InvertDiagBlocksLowerTriangular" | custom-call | tf_op jit(solution)/shard_map/jit(_solve_triangular)/triangular_solve | solution.py:107
  469.6 16.5 %fusion.29 = bf16[3,256,1024]{2,1,0:T(8,128)(2,1)S(1)} fusion(f32[1024,1024]{1,0:T(8,128)} %convolution_dynamic-update-slice_fusion, f32[3,256,1024,1]{2,1,0,3:T(8,128)S(1)} %fusion.27, f32[1024]{0:T(1024)S(1)} %bitcast.431, f32[3,256]{1,0:T(4,128)S(1)} %get-tuple-element.148, f32[1024]{0:T(1024)S(1)} %bitcast.429, f32[3,256]{1,0:T(4,128)S(1)} %get-tuple-element.149, ...), kind=kOutput, calls=%fused_computation.40 | convolution fusion | flops 9674686464 | bytes 8927244 | tf_op jit(solution)/shard_map/snb,cb->snc/dot_general | solution.py:113
  529.1 10.8 %all-to-all-start.1 = ((bf16[64,3,4,1,1024]{4,2,1,3,0:T(4,128)(2,1)}), bf16[64,3,4,1,1024]{4,2,1,3,0:T(4,128)(2,1)S(1)}, u32[]{:S(2)}, u32[]{:S(2)}) async-start(bf16[64,3,4,1,1024]{4,2,1,3,0:T(4,128)(2,1)} %constant_dynamic-update-slice_fusion.25), calls=%async_computation.1 | async-start | bytes 3145728 | tf_op jit(solution)/shard_map/all_to_all | solution.py:123
  548.3 31.4 %all-to-all-done.1 = bf16[64,3,4,1,1024]{4,2,1,3,0:T(4,128)(2,1)S(1)} async-done(((bf16[64,3,4,1,1024]{4,2,1,3,0:T(4,128)(2,1)}), bf16[64,3,4,1,1024]{4,2,1,3,0:T(4,128)(2,1)S(1)}, u32[]{:S(2)}, u32[]{:S(2)}) %all-to-all-start.1) | async-done | bytes 1572896 | tf_op jit(solution)/shard_map/all_to_all | solution.py:123
  (213 shorter events, 191.7 us)
Async XLA Ops:
  7.2 532.8 %copy-start = (f32[1024,128]{1,0:T(8,128)S(1)}, f32[1024,128]{1,0:T(8,128)}, u32[]{:S(2)}) copy-start(f32[1024,128]{1,0:T(8,128)} %param.20) | copy-start | bytes 1572868
  7.2 5.9 copy-start.10
  7.2 5.8 copy-start.9
  7.2 53.9 %all-gather.5.cloned.1.call-start = ((), (), s32[]{:S(2)}) async-start(), calls=%async_computation.2 | async-start | bytes 2621440 | tf_op jit(solution)/shard_map/all_gather | solution.py:90
  9.9 87.9 %all-gather.9.cloned.1.call-start = ((), (), s32[]{:S(2)}) async-start(), calls=%async_computation.4 | async-start | bytes 2621440 | tf_op jit(solution)/shard_map/all_gather | solution.py:89
  16.8 6.3 %copy-start.7 = (s32[2,1024]{1,0:T(2,128)S(1)}, s32[2,1024]{1,0:T(2,128)}, u32[]{:S(2)}) copy-start(s32[2,1024]{1,0:T(2,128)} %param.19) | copy-start | bytes 24580
  16.8 6.3 %copy-start.8 = (s32[3,2,256]{2,1,0:T(2,128)S(1)}, s32[3,2,256]{2,1,0:T(2,128)}, u32[]{:S(2)}) copy-start(s32[3,2,256]{2,1,0:T(2,128)} %param.18) | copy-start | bytes 18436
  16.8 6.3 %copy-start.6 = (s32[64,3]{0,1:T(4,128)S(1)}, s32[64,3]{0,1:T(4,128)}, u32[]{:S(2)}) copy-start(s32[64,3]{0,1:T(4,128)} %param.11) | copy-start | bytes 2308
  18.1 448.0 %all-to-all-start = ((bf16[3,4,256,256]{3,2,0,1:T(8,128)(2,1)}), bf16[3,4,256,256]{3,2,0,1:T(8,128)(2,1)S(1)}, u32[]{:S(2)}, u32[]{:S(2)}) async-start(bf16[3,4,256,256]{3,2,0,1:T(8,128)(2,1)} %copy.149), calls=%async_computation | async-start | bytes 3145728 | tf_op jit(solution)/shard_map/all_to_all | solution.py:95
  119.3 2.0 copy-start.2
  438.9 3.4 copy-start.1
  486.1 3.5 copy-start.3
  529.1 50.6 %all-to-all-start.1 = ((bf16[64,3,4,1,1024]{4,2,1,3,0:T(4,128)(2,1)}), bf16[64,3,4,1,1024]{4,2,1,3,0:T(4,128)(2,1)S(1)}, u32[]{:S(2)}, u32[]{:S(2)}) async-start(bf16[64,3,4,1,1024]{4,2,1,3,0:T(4,128)(2,1)} %constant_dynamic-update-slice_fusion.25), calls=%async_computation.1 | async-start | bytes 3145728 | tf_op jit(solution)/shard_map/all_to_all | solution.py:123
  539.9 45.9 %all-gather.7.cloned.1.call-start = ((), (), s32[]{:S(2)}) async-start(), calls=%async_computation.3 | async-start | bytes 1310720 | tf_op jit(solution)/shard_map/all_gather | solution.py:39
  579.7 1.2 copy-start.4
  585.8 5.9 copy-start.5
Sparse Core Ops, SparseCore 0:
  10.0 51.0 all-gather.4
  63.5 34.2 all-gather.8
  546.6 26.3 all-gather.6
